TPU v7x, 256 devices: a whole 4x4x8 slice. The times are simulated.
256 devices in a mesh: row: 32 (over y, z), col: 8 (over x, core).
Axes of the slice: x: 4, y: 4, z: 8, core: 2. Of those that a mesh axis runs over, the one named last changes fastest.
Arguments:
- acts: bfloat16 [6144, 28672], P('col', 'row'), may hold values from -12 to 12
- out_grad: bfloat16 [6144, 8192], P('row', 'col'), may hold values from -12 to 12
- lengths: int32 [8], replicated, may hold values from 1 to 768, 4800 in all
Outputs:
- weight_grad: bfloat16 [28672, 8192], P('row', 'col')
- norms: float32 [8], replicated
All inputs are finite; a program needn't handle non-finite values.
Results may differ from a plain program's by a relative error of at most 0.0013.
Values may be sent and summed in bfloat16 or wider, within the bound.
No kernel may reach another device: no remote copies, remote signals or barrier semaphores. Data moves between devices by JAX's collectives and lax.ppermute only.
A program may use at most 128 MiB of HBM per device.

v0:
```python
import jax
import jax.numpy as jnp
from jax import lax
from jax.sharding import PartitionSpec as P

FF = 28672
D = 8192


def exchange_sum(value, axis, shifts):
    size = lax.axis_size(axis)
    parts = [value]
    for shift in shifts:
        parts.append(lax.ppermute(value, axis, [(i, i ^ shift) for i in range(size)]))
    while len(parts) > 1:
        parts = [parts[i] + parts[i + 1] for i in range(0, len(parts), 2)]
    return parts[0]


def sum_everywhere(value):
    value = exchange_sum(value, "col", (1,))
    value = exchange_sum(value, "col", (2, 4, 6))
    value = exchange_sum(value, "row", (8, 16, 24))
    value = exchange_sum(value, "row", (1, 2, 3))
    return exchange_sum(value, "row", (4,))


def body(acts, out_grad, lengths):
    n_row = lax.axis_size("row")
    row_idx = lax.axis_index("row")
    own_rows = out_grad.shape[0]
    tokens = own_rows * n_row
    seqs = lengths.shape[0]
    seq_len = tokens // seqs
    positions = row_idx * own_rows + jnp.arange(own_rows, dtype=jnp.int32)
    seq_of = positions // seq_len
    limit = jnp.sum(
        jnp.where(
            seq_of[:, None] == jnp.arange(seqs, dtype=jnp.int32)[None, :], lengths[None, :], 0
        ),
        axis=1,
    )
    live = positions % seq_len < limit
    own_grads = jnp.where(live[:, None], out_grad, jnp.zeros_like(out_grad))
    grads = lax.all_gather(own_grads, "row", axis=0, tiled=True)
    act_full = lax.all_gather(acts, "col", axis=0, tiled=True)
    products = []
    sums = []
    for seq in range(seqs):
        act_rows = act_full[seq * seq_len : (seq + 1) * seq_len]
        grad_rows = grads[seq * seq_len : (seq + 1) * seq_len]
        product = lax.dot_general(
            act_rows, grad_rows, (((0,), (0,)), ((), ())), preferred_element_type=jnp.float32
        )
        products.append(product)
        sums.append(jnp.sum(product * product))
    squares = sum_everywhere(jnp.stack(sums))
    norms = jnp.sqrt(squares / (float(FF) * float(D) * float(seq_len)))
    scale = 1.0 / (norms + 0.1)
    total = scale[0] * products[0]
    for seq in range(1, seqs):
        total = total + scale[seq] * products[seq]
    weight_grad = (total / jnp.sqrt(jnp.float32(tokens))).astype(jnp.bfloat16)
    return (weight_grad, norms)


def solution(mesh):
    placed = (P("col", "row"), P("row", "col"), P())
    return jax.shard_map(
        body, mesh=mesh, in_specs=placed, out_specs=(P("row", "col"), P()), check_vma=False
    )
```

profile of v0, /device:TPU:8, one launch (start us, length us, event | category | flops | bytes accessed | tf_op | source)
XLA Modules:
  0.0 299.2 jit_solution(15958608026676265516)
XLA Ops:
  7.2 0.0 all-gather.5.cloned.1.call-start
  7.2 0.7 all-gather.5.cloned.1.call-update
  7.9 0.0 all-gather.3.cloned.1.call-start
  8.0 0.7 select_reduce_fusion
  8.7 1.8 broadcast_select_fusion
  10.6 0.0 all-gather.3.cloned.1.call-update
  10.6 65.3 %all-gather.5.cloned.1.call-done = bf16[6144,896]{1,0:T(8,128)(2,1)} async-done(((bf16[768,896]{1,0:T(8,128)(2,1)}), bf16[6144,896]{1,0:T(8,128)(2,1)}) %all-gather.5.cloned.1.call-update) | async-done | bytes 11010064 | tf_op jit(solution)/shard_map/all_gather | solution.py:46
  75.9 121.2 %all-gather.3.cloned.1.call-done = bf16[6144,1024]{1,0:T(8,128)(2,1)} async-done(((bf16[192,1024]{1,0:T(8,128)(2,1)}), bf16[6144,1024]{1,0:T(8,128)(2,1)}) %all-gather.3.cloned.1.call-update) | async-done | bytes 12582928 | tf_op jit(solution)/shard_map/all_gather | solution.py:45
  197.1 0.0 slice-start
  197.1 0.0 slice-start.1
  197.1 0.0 copy-start
  197.1 6.3 %multiply_reduce_fusion = (f32[]{:T(128)}, f32[1024,896]{1,0:T(8,128)}) fusion(bf16[6144,896]{1,0:T(8,128)(2,1)} %all-gather.5.cloned.1.call-done, bf16[6144,1024]{1,0:T(8,128)(2,1)} %all-gather.3.cloned.1.call-done), kind=kOutput, calls=%fused_computation.1 | convolution fusion | flops 1411121152 | bytes 6619140 | tf_op jit(solution)/shard_map/dot_general | solution.py:52
  203.3 0.0 slice-start.2
  203.3 7.0 %multiply_reduce_fusion.1 = (f32[]{:T(128)}, f32[1024,896]{1,0:T(8,128)}) fusion(bf16[6144,896]{1,0:T(8,128)(2,1)} %all-gather.5.cloned.1.call-done, bf16[6144,1024]{1,0:T(8,128)(2,1)} %all-gather.3.cloned.1.call-done), kind=kOutput, calls=%fused_computation.2 | convolution fusion | flops 1411121152 | bytes 6619140 | tf_op jit(solution)/shard_map/dot_general | solution.py:52
  210.4 0.0 slice-done
  210.4 0.0 slice-done.1
  210.4 0.0 copy-done
  210.4 0.0 slice-done.2
  210.4 4.3 %multiply_reduce_fusion.2 = (f32[]{:T(128)}, f32[1024,896]{1,0:T(8,128)}) fusion(bf16[6144,896]{1,0:T(8,128)(2,1)S(1)} %copy-done, bf16[6144,1024]{1,0:T(8,128)(2,1)S(1)} %bitcast.19), kind=kOutput, calls=%fused_computation.3 | convolution fusion | flops 1411121152 | bytes 6619140 | tf_op jit(solution)/shard_map/dot_general | solution.py:52
  214.7 4.3 %multiply_reduce_fusion.3 = (f32[]{:T(128)}, f32[1024,896]{1,0:T(8,128)}) fusion(bf16[6144,896]{1,0:T(8,128)(2,1)S(1)} %copy-done, bf16[6144,1024]{1,0:T(8,128)(2,1)S(1)} %bitcast.19), kind=kOutput, calls=%fused_computation.4 | convolution fusion | flops 1411121152 | bytes 6619140 | tf_op jit(solution)/shard_map/dot_general | solution.py:52
  219.0 4.4 %multiply_reduce_fusion.4 = (f32[]{:T(128)}, f32[1024,896]{1,0:T(8,128)}) fusion(bf16[6144,896]{1,0:T(8,128)(2,1)S(1)} %copy-done, bf16[6144,1024]{1,0:T(8,128)(2,1)S(1)} %bitcast.19), kind=kOutput, calls=%fused_computation.5 | convolution fusion | flops 1411121152 | bytes 6619140 | tf_op jit(solution)/shard_map/dot_general | solution.py:52
  223.4 4.4 %multiply_reduce_fusion.5 = (f32[]{:T(128)}, f32[1024,896]{1,0:T(8,128)}) fusion(bf16[6144,896]{1,0:T(8,128)(2,1)S(1)} %copy-done, bf16[6144,1024]{1,0:T(8,128)(2,1)S(1)} %bitcast.19), kind=kOutput, calls=%fused_computation.6 | convolution fusion | flops 1411121152 | bytes 6619140 | tf_op jit(solution)/shard_map/dot_general | solution.py:52
  227.8 4.5 %multiply_reduce_fusion.6 = (f32[]{:T(128)}, f32[1024,896]{1,0:T(8,128)}) fusion(bf16[6144,896]{1,0:T(8,128)(2,1)S(1)} %copy-done, bf16[6144,1024]{1,0:T(8,128)(2,1)S(1)} %bitcast.19), kind=kOutput, calls=%fused_computation.7 | convolution fusion | flops 1411121152 | bytes 6619140 | tf_op jit(solution)/shard_map/dot_general | solution.py:52
  232.3 4.2 %multiply_reduce_fusion.7 = (f32[]{:T(128)}, f32[1024,896]{1,0:T(8,128)}) fusion(bf16[6144,896]{1,0:T(8,128)(2,1)S(1)} %copy-done, bf16[6144,1024]{1,0:T(8,128)(2,1)S(1)} %bitcast.19), kind=kOutput, calls=%fused_computation.8 | convolution fusion | flops 1411121152 | bytes 6619140 | tf_op jit(solution)/shard_map/dot_general | solution.py:52
  236.6 5.1 %stack.35 = f32[8]{0:T(128)S(1)} concatenate(f32[1]{0:T(128)} %bitcast, f32[1]{0:T(128)} %bitcast.1, f32[1]{0:T(128)} %bitcast.2, f32[1]{0:T(128)} %bitcast.3, f32[1]{0:T(128)} %bitcast.4, f32[1]{0:T(128)} %bitcast.5, f32[1]{0:T(128)} %bitcast.6, f32[1]{0:T(128)} %bitcast.7), dimensions={0} | concatenate | bytes 64 | tf_op jit(solution)/shard_map/stack | solution.py:57
  241.7 0.0 collective-permute-start
  241.8 1.1 collective-permute-done
  242.9 2.7 collective-permute-start.3
  245.6 0.8 collective-permute-start.2
  246.4 0.6 collective-permute-start.1
  247.0 0.7 collective-permute-done.3
  247.7 3.0 collective-permute-done.2
  250.7 0.0 collective-permute-done.1
  250.7 1.3 collective-permute-start.6
  252.0 2.7 collective-permute-start.5
  254.6 0.2 collective-permute-start.4
  254.9 0.0 collective-permute-done.6
  254.9 2.2 collective-permute-done.5
  257.0 1.2 collective-permute-done.4
  258.2 3.0 collective-permute-start.9
  261.2 0.0 collective-permute-start.8
  261.2 1.4 collective-permute-start.7
  262.6 1.0 collective-permute-done.9
  263.6 2.1 collective-permute-done.8
  265.7 0.0 collective-permute-done.7
  265.7 2.0 collective-permute-start.10
  267.7 5.5 %collective-permute-done.10 = f32[8]{0:T(128)S(1)} collective-permute-done((f32[8]{0:T(128)S(1)}, f32[8]{0:T(128)S(1)}, u32[]{:S(2)}, u32[]{:S(2)}) %collective-permute-start.10) | collective-permute-done | bytes 64 | tf_op jit(solution)/shard_map/ppermute | solution.py:14
  273.2 0.5 add_divide_fusion
  273.8 0.7 fusion.28
  274.4 15.5 %fusion = bf16[896,1024]{0,1:T(8,128)(2,1)S(1)} fusion(f32[1024,896]{1,0:T(8,128)} %get-tuple-element.31, f32[]{:T(128)} %bitcast.15, f32[1024,896]{1,0:T(8,128)} %get-tuple-element.29, f32[]{:T(128)} %bitcast.14, f32[1024,896]{1,0:T(8,128)} %get-tuple-element.27, f32[]{:T(128)} %bitcast.13, f32[1024,896]{1,0:T(8,128)} %get-tuple-element.25, f32[]{:T(128)} %bitcast.12, ...), kind=kLoop, calls=%fused_computation.9 | loop fusion | flops 15597568 | bytes 31195168 | tf_op jit(solution)/shard_map/convert_element_type | solution.py:63
  289.9 2.4 copy.6
  (7 shorter events, 0.1 us)
Async XLA Ops:
  7.2 68.7 %all-gather.5.cloned.1.call-start = ((), (), s32[]{:S(2)}) async-start(), calls=%async_computation.1 | async-start | bytes 12386304 | tf_op jit(solution)/shard_map/all_gather | solution.py:46
  7.9 189.2 %all-gather.3.cloned.1.call-start = ((), (), s32[]{:S(2)}) async-start(), calls=%async_computation | async-start | bytes 12976128 | tf_op jit(solution)/shard_map/all_gather | solution.py:45
  197.1 13.3 %slice-start = ((s8[12582912]{0:T(1024)(128)(4,1)}), s8[4194304]{0:T(1024)(128)(4,1)S(1)}, s32[]{:S(2)}) async-start(s8[12582912]{0:T(1024)(128)(4,1)} %bitcast.18), calls=%async_computation.2 | async-start | bytes 8388608
  197.1 13.3 %slice-start.1 = ((s8[12582912]{0:T(1024)(128)(4,1)}), s8[4194304]{0:T(1024)(128)(4,1)S(1)}, s32[]{:S(2)}) async-start(s8[12582912]{0:T(1024)(128)(4,1)} %bitcast.18), calls=%async_computation.3 | async-start | bytes 8388608
  197.1 13.3 %copy-start = (bf16[6144,896]{1,0:T(8,128)(2,1)S(1)}, bf16[6144,896]{1,0:T(8,128)(2,1)}, u32[]{:S(2)}) copy-start(bf16[6144,896]{1,0:T(8,128)(2,1)} %all-gather.5.cloned.1.call-done) | copy-start | bytes 33030148
  203.3 7.1 %slice-start.2 = ((s8[12582912]{0:T(1024)(128)(4,1)}), s8[4194304]{0:T(1024)(128)(4,1)S(1)}, s32[]{:S(2)}) async-start(s8[12582912]{0:T(1024)(128)(4,1)} %bitcast.18), calls=%async_computation.4 | async-start | bytes 8388608
  241.7 1.2 collective-permute-start
  242.9 4.8 %collective-permute-start.3 = (f32[8]{0:T(128)S(1)}, f32[8]{0:T(128)S(1)}, u32[]{:S(2)}, u32[]{:S(2)}) collective-permute-start(f32[8]{0:T(128)S(1)} %add.93), channel_id=1, source_target_pairs={{0,6},{1,7},{2,4},{3,5},{4,2},{5,3},{6,0},{7,1},{8,14},{9,15},{10,... | collective-permute-start | bytes 104 | tf_op jit(solution)/shard_map/ppermute | solution.py:14
  245.6 5.1 %collective-permute-start.2 = (f32[8]{0:T(128)S(1)}, f32[8]{0:T(128)S(1)}, u32[]{:S(2)}, u32[]{:S(2)}) collective-permute-start(f32[8]{0:T(128)S(1)} %add.93), channel_id=1, source_target_pairs={{0,4},{1,5},{2,6},{3,7},{4,0},{5,1},{6,2},{7,3},{8,12},{9,13},{10,... | collective-permute-start | bytes 104 | tf_op jit(solution)/shard_map/ppermute | solution.py:14
  246.4 4.2 %collective-permute-start.1 = (f32[8]{0:T(128)S(1)}, f32[8]{0:T(128)S(1)}, u32[]{:S(2)}, u32[]{:S(2)}) collective-permute-start(f32[8]{0:T(128)S(1)} %add.93), channel_id=1, source_target_pairs={{0,2},{1,3},{2,0},{3,1},{4,6},{5,7},{6,4},{7,5},{8,10},{9,11},{10,... | collective-permute-start | bytes 104 | tf_op jit(solution)/shard_map/ppermute | solution.py:14
  250.7 4.2 %collective-permute-start.6 = (f32[8]{0:T(128)S(1)}, f32[8]{0:T(128)S(1)}, u32[]{:S(2)}, u32[]{:S(2)}) collective-permute-start(f32[8]{0:T(128)S(1)} %add_add_fusion.2), channel_id=1, source_target_pairs={{0,192},{8,200},{16,208},{24,216},{32,224},{40,232},{48,240},{56,2... | collective-permute-start | bytes 104 | tf_op jit(solution)/shard_map/ppermute | solution.py:14
  252.0 5.1 %collective-permute-start.5 = (f32[8]{0:T(128)S(1)}, f32[8]{0:T(128)S(1)}, u32[]{:S(2)}, u32[]{:S(2)}) collective-permute-start(f32[8]{0:T(128)S(1)} %add_add_fusion.2), channel_id=1, source_target_pairs={{0,128},{8,136},{16,144},{24,152},{32,160},{40,168},{48,176},{56,1... | collective-permute-start | bytes 104 | tf_op jit(solution)/shard_map/ppermute | solution.py:14
  254.6 3.6 %collective-permute-start.4 = (f32[8]{0:T(128)S(1)}, f32[8]{0:T(128)S(1)}, u32[]{:S(2)}, u32[]{:S(2)}) collective-permute-start(f32[8]{0:T(128)S(1)} %add_add_fusion.2), channel_id=1, source_target_pairs={{0,64},{8,72},{16,80},{24,88},{32,96},{40,104},{48,112},{56,120},{... | collective-permute-start | bytes 104 | tf_op jit(solution)/shard_map/ppermute | solution.py:14
  258.2 5.4 %collective-permute-start.9 = (f32[8]{0:T(128)S(1)}, f32[8]{0:T(128)S(1)}, u32[]{:S(2)}, u32[]{:S(2)}) collective-permute-start(f32[8]{0:T(128)S(1)} %add_add_fusion.1), channel_id=1, source_target_pairs={{0,24},{8,16},{16,8},{24,0},{32,56},{40,48},{48,40},{56,32},{64,88... | collective-permute-start | bytes 104 | tf_op jit(solution)/shard_map/ppermute | solution.py:14
  261.2 4.5 %collective-permute-start.8 = (f32[8]{0:T(128)S(1)}, f32[8]{0:T(128)S(1)}, u32[]{:S(2)}, u32[]{:S(2)}) collective-permute-start(f32[8]{0:T(128)S(1)} %add_add_fusion.1), channel_id=1, source_target_pairs={{0,16},{8,24},{16,0},{24,8},{32,48},{40,56},{48,32},{56,40},{64,80... | collective-permute-start | bytes 104 | tf_op jit(solution)/shard_map/ppermute | solution.py:14
  261.2 4.5 %collective-permute-start.7 = (f32[8]{0:T(128)S(1)}, f32[8]{0:T(128)S(1)}, u32[]{:S(2)}, u32[]{:S(2)}) collective-permute-start(f32[8]{0:T(128)S(1)} %add_add_fusion.1), channel_id=1, source_target_pairs={{0,8},{8,0},{16,24},{24,16},{32,40},{40,32},{48,56},{56,48},{64,72... | collective-permute-start | bytes 104 | tf_op jit(solution)/shard_map/ppermute | solution.py:14
  265.7 7.6 %collective-permute-start.10 = (f32[8]{0:T(128)S(1)}, f32[8]{0:T(128)S(1)}, u32[]{:S(2)}, u32[]{:S(2)}) collective-permute-start(f32[8]{0:T(128)S(1)} %add_add_fusion), channel_id=1, source_target_pairs={{0,32},{8,40},{16,48},{24,56},{32,0},{40,8},{48,16},{56,24},{64,96... | collective-permute-start | bytes 104 | tf_op jit(solution)/shard_map/ppermute | solution.py:14
Sparse Core Ops, SparseCore 0:
  9.8 66.0 all-gather.4
  79.1 117.9 all-gather.2
where the time goes:
time: 299 us
  waiting for transfers between devices  204 us (68%)
  matrix products  39.5 us (13%)
  other arithmetic  18.6 us (6%)
  starting transfers between devices  14.8 us (5%)
  between operations  14.1 us (5%)
  local copies, waits for them, and re-layouts  8.23 us (3%)
    all_gather x1, waiting for transfers between devices, body(): grads = lax.all_gather(own_grads, 'row', axis=0, tiled=True)  121 us
    all_gather x1, waiting for transfers between devices, body(): act_full = lax.all_gather(acts, 'col', axis=0, tiled=True)  65.3 us
    dot_general x8, matrix products, body(): lax.dot_general(act_rows, grad_rows, (((0,), (0,)), ((), ())), preferred_...  39.5 us
    ppermute x11, waiting for transfers between devices, exchange_sum(): lax.ppermute(value, axis, [(i, i ^ shift) for i in range(size)])  16.8 us
    convert_element_type x1, other arithmetic, body(): weight_grad = (total / jnp.sqrt(jnp.float32(tokens))).astype(jnp.bfloat16)  15.5 us
    ppermute x11, starting transfers between devices, exchange_sum(): lax.ppermute(value, axis, [(i, i ^ shift) for i in range(size)])  14.7 us
  transfers between devices with their start and end apart: 13, of which 10 were waited for; matrix products, arithmetic and copies ran while one was open for 1% of the time, Pallas kernels for 0%

commit v1 on v0

--- a/solution.py
+++ b/solution.py
@@ -5,6 +5,12 @@
 
 FF = 28672
 D = 8192
+
+
+def in_order(parts, dim):
+    parts = jnp.moveaxis(parts, 0, dim)
+    shape = parts.shape
+    return parts.reshape(*shape[:dim], shape[dim] * shape[dim + 1], *shape[dim + 2 :])
 
 
 def exchange_sum(value, axis, shifts):
@@ -43,7 +49,19 @@
     live = positions % seq_len < limit
     own_grads = jnp.where(live[:, None], out_grad, jnp.zeros_like(out_grad))
     grads = lax.all_gather(own_grads, "row", axis=0, tiled=True)
-    act_full = lax.all_gather(acts, "col", axis=0, tiled=True)
+    length = lax.axis_size("col")
+    pairs = [(i_2, (i_2 + 1) % length) for i_2 in range(length)]
+    back = [(b, a) for a, b in pairs]
+    lower, upper = ([], [])
+    for turn in range(length - 1):
+        if turn % 2 == 0:
+            lower.append(lax.ppermute(lower[-1] if lower else acts, "col", pairs))
+        else:
+            upper.append(lax.ppermute(upper[-1] if upper else acts, "col", back))
+    blocks = jnp.stack([*lower[::-1], acts, *upper])
+    shift_2 = lax.axis_index("col") - len(lower)
+    blocks = blocks[(jnp.arange(length) - shift_2) % length]
+    act_full = in_order(blocks, 0)
     products = []
     sums = []
     for seq in range(seqs):

time: 299 us -> 232 us (0.78)
  waiting for transfers between devices: 204 us -> 104 us
  local copies, waits for them, and re-layouts: 8.23 us -> 30.9 us
  starting transfers between devices: 14.8 us -> 23.3 us
    all_gather x1, waiting for transfers between devices: 121 us -> 20.6 us  [body(): grads = lax.all_gather(own_grads, 'row', axis=0, tiled=True)]
    ppermute x0 -> x7, waiting for transfers between devices: none -> 67 us  [the longest x4 66.7 us: body(): lower.append(lax.ppermute(lower[-1] if lower else acts, 'col', pairs))]
    all_gather x1 -> x0, waiting for transfers between devices: 65.3 us -> none  [body(): act_full = lax.all_gather(acts, 'col', axis=0, tiled=True)]
    unnamed x9 -> x17, local copies, waits for them, and re-layouts: 2.42 us -> 13.6 us
    gather x0 -> x1, local copies, waits for them, and re-layouts: none -> 10.4 us  [body(): blocks = blocks[(jnp.arange(length) - shift_2) % length]]
    ppermute x0 -> x7, starting transfers between devices: none -> 8.51 us  [the longest x3 8.48 us: body(): upper.append(lax.ppermute(upper[-1] if upper else acts, 'col', back))]
  transfers between devices with their start and end apart: 13 -> 19, of which waited for: 10 -> 15; matrix products, arithmetic and copies ran while one was open for 1% -> 10% of each run, Pallas kernels for 0% -> 0%
where the time goes in v1:
time: 232 us; the launch traced here: 231 us
  waiting for transfers between devices  104 us (45%)
  matrix products  38.1 us (16%)
  local copies, waits for them, and re-layouts  30.9 us (13%)
  starting transfers between devices  23.3 us (10%)
  other arithmetic  20.7 us (9%)
  between operations  14.1 us (6%)
    ppermute x4, waiting for transfers between devices, body(): lower.append(lax.ppermute(lower[-1] if lower else acts, 'col', pairs))  66.7 us
    dot_general x8, matrix products, body(): lax.dot_general(act_rows, grad_rows, (((0,), (0,)), ((), ())), preferred_...  38.1 us
    all_gather x1, waiting for transfers between devices, body(): grads = lax.all_gather(own_grads, 'row', axis=0, tiled=True)  20.6 us
    convert_element_type x1, other arithmetic, body(): weight_grad = (total / jnp.sqrt(jnp.float32(tokens))).astype(jnp.bfloat16)  17.5 us
    ppermute x11, waiting for transfers between devices, exchange_sum(): lax.ppermute(value, axis, [(i, i ^ shift) for i in range(size)])  16.8 us
    ppermute x11, starting transfers between devices, exchange_sum(): lax.ppermute(value, axis, [(i, i ^ shift) for i in range(size)])  14.7 us
    unnamed x17, local copies, waits for them, and re-layouts  13.6 us
    gather x1, local copies, waits for them, and re-layouts, body(): blocks = blocks[(jnp.arange(length) - shift_2) % length]  10.4 us
  transfers between devices with their start and end apart: 19, of which 15 were waited for; matrix products, arithmetic and copies ran while one was open for 10% of the time, Pallas kernels for 0%

profile of v1, /device:TPU:8, one launch (start us, length us, event | category | flops | bytes accessed | tf_op | source)
XLA Modules:
  0.0 231.4 jit_solution(12579386456246285696)
XLA Ops:
  7.2 0.0 all-gather.2.cloned.1.call-start
  7.2 0.7 select_reduce_fusion
  8.0 1.9 broadcast_select_fusion
  9.8 0.0 all-gather.2.cloned.1.call-update
  9.9 0.0 collective-permute-start
  9.9 19.1 %collective-permute-done = bf16[768,896]{1,0:T(8,128)(2,1)S(1)} collective-permute-done((bf16[768,896]{1,0:T(8,128)(2,1)}, bf16[768,896]{1,0:T(8,128)(2,1)S(1)}, u32[]{:S(2)}, u32[]{:S(2)}) %collective-permute-start) | collective-permute-done | bytes 1376288 | tf_op jit(solution)/shard_map/ppermute | solution.py:58
  29.0 0.0 collective-permute-start.1
  29.0 3.0 %collective-permute-start.4 = (bf16[768,896]{1,0:T(8,128)(2,1)}, bf16[768,896]{1,0:T(8,128)(2,1)S(1)}, u32[]{:S(2)}, u32[]{:S(2)}) collective-permute-start(bf16[768,896]{1,0:T(8,128)(2,1)} %param.3), channel_id=1, source_target_pairs={{1,0},{2,1},{3,2},{4,3},{5,4},{6,5},{7,6},{0,7},{9,8},{10,9},{11,1... | collective-permute-start | bytes 4128776 | tf_op jit(solution)/shard_map/ppermute | solution.py:60
  32.0 16.0 %collective-permute-done.1 = bf16[768,896]{1,0:T(8,128)(2,1)S(1)} collective-permute-done((bf16[768,896]{1,0:T(8,128)(2,1)S(1)}, bf16[768,896]{1,0:T(8,128)(2,1)S(1)}, u32[]{:S(2)}, u32[]{:S(2)}) %collective-permute-start.1) | collective-permute-done | bytes 1376288 | tf_op jit(solution)/shard_map/ppermute | solution.py:58
  48.0 0.0 collective-permute-start.2
  48.0 0.1 collective-permute-done.4
  48.1 0.9 copy-done.2
  49.1 2.3 collective-permute-start.5
  51.4 15.7 %collective-permute-done.2 = bf16[768,896]{1,0:T(8,128)(2,1)} collective-permute-done((bf16[768,896]{1,0:T(8,128)(2,1)S(1)}, bf16[768,896]{1,0:T(8,128)(2,1)}, u32[]{:S(2)}, u32[]{:S(2)}) %collective-permute-start.2) | collective-permute-done | bytes 1376288 | tf_op jit(solution)/shard_map/ppermute | solution.py:58
  67.0 0.0 collective-permute-start.3
  67.1 0.1 collective-permute-done.5
  67.2 3.2 %collective-permute-start.6 = (bf16[768,896]{1,0:T(8,128)(2,1)}, bf16[768,896]{1,0:T(8,128)(2,1)S(1)}, u32[]{:S(2)}, u32[]{:S(2)}) collective-permute-start(bf16[768,896]{1,0:T(8,128)(2,1)} %collective-permute-done.5), channel_id=1, source_target_pairs={{1,0},{2,1},{3,2},{4,3},{5,4},{6,5},{7,6},{0,7},{9,8},{10,9},{11,1... | collective-permute-start | bytes 4128776 | tf_op jit(solution)/shard_map/ppermute | solution.py:60
  70.4 15.9 %collective-permute-done.3 = bf16[768,896]{1,0:T(8,128)(2,1)} collective-permute-done((bf16[768,896]{1,0:T(8,128)(2,1)}, bf16[768,896]{1,0:T(8,128)(2,1)}, u32[]{:S(2)}, u32[]{:S(2)}) %collective-permute-start.3) | collective-permute-done | bytes 1376288 | tf_op jit(solution)/shard_map/ppermute | solution.py:58
  86.3 2.6 %bitcast_dynamic-update-slice_fusion.7 = bf16[8,768,896]{2,1,0:T(8,128)(2,1)} fusion(bf16[768,896]{1,0:T(8,128)(2,1)} %collective-permute-done.3), kind=kLoop, calls=%fused_computation.41 | loop fusion | bytes 2752512
  88.9 2.6 %bitcast_dynamic-update-slice_fusion.6 = bf16[8,768,896]{2,1,0:T(8,128)(2,1)} fusion(bf16[8,768,896]{2,1,0:T(8,128)(2,1)} %bitcast_dynamic-update-slice_fusion.7, bf16[768,896]{1,0:T(8,128)(2,1)} %collective-permute-done.2), kind=kLoop, calls=%fused_computation.40 | loop fusion | bytes 2752512
  91.6 1.2 bitcast_dynamic-update-slice_fusion.5
  92.8 1.2 bitcast_dynamic-update-slice_fusion.4
  94.0 1.2 bitcast_dynamic-update-slice_fusion.3
  95.2 1.2 bitcast_dynamic-update-slice_fusion.2
  96.4 2.6 %bitcast_dynamic-update-slice_fusion.1 = bf16[8,768,896]{2,1,0:T(8,128)(2,1)} fusion(bf16[8,768,896]{2,1,0:T(8,128)(2,1)} %bitcast_dynamic-update-slice_fusion.2, bf16[768,896]{1,0:T(8,128)(2,1)} %collective-permute-done.5), kind=kLoop, calls=%fused_computation.35 | loop fusion | bytes 2752512
  98.9 0.0 collective-permute-done.6
  98.9 1.2 bitcast_dynamic-update-slice_fusion
  100.2 10.4 %gather_fusion = bf16[8,768,896]{2,1,0:T(8,128)(2,1)} fusion(bf16[8,768,896]{2,1,0:T(8,128)(2,1)} %bitcast_dynamic-update-slice_fusion, s32[1024]{0:T(1024)S(1)} %pad_clamp_fusion), kind=kCustom, calls=%fused_computation | custom fusion | bytes 22020128 | tf_op jit(solution)/shard_map/gather | solution.py:63
  110.5 20.6 %all-gather.2.cloned.1.call-done = bf16[6144,1024]{1,0:T(8,128)(2,1)} async-done(((bf16[192,1024]{1,0:T(8,128)(2,1)}), bf16[6144,1024]{1,0:T(8,128)(2,1)}) %all-gather.2.cloned.1.call-update) | async-done | bytes 12582928 | tf_op jit(solution)/shard_map/all_gather | solution.py:51
  131.1 6.0 %multiply_reduce_fusion.1 = (f32[]{:T(128)}, f32[896,1024]{1,0:T(8,128)}) fusion(bf16[6144,1024]{1,0:T(8,128)(2,1)} %all-gather.2.cloned.1.call-done, bf16[8,768,896]{2,1,0:T(8,128)(2,1)} %gather_fusion), kind=kOutput, calls=%fused_computation.3 | convolution fusion | flops 1411121152 | bytes 6619140 | tf_op jit(solution)/shard_map/dot_general | solution.py:70
  137.1 0.0 copy-done
  137.1 5.8 %multiply_reduce_fusion.2 = (f32[]{:T(128)}, f32[896,1024]{1,0:T(8,128)}) fusion(bf16[6144,1024]{1,0:T(8,128)(2,1)} %all-gather.2.cloned.1.call-done, bf16[8,768,896]{2,1,0:T(8,128)(2,1)S(1)} %copy-done), kind=kOutput, calls=%fused_computation.4 | convolution fusion | flops 1411121152 | bytes 6619140 | tf_op jit(solution)/shard_map/dot_general | solution.py:70
  142.8 5.6 %multiply_reduce_fusion.3 = (f32[]{:T(128)}, f32[896,1024]{1,0:T(8,128)}) fusion(bf16[6144,1024]{1,0:T(8,128)(2,1)} %all-gather.2.cloned.1.call-done, bf16[8,768,896]{2,1,0:T(8,128)(2,1)S(1)} %copy-done), kind=kOutput, calls=%fused_computation.5 | convolution fusion | flops 1411121152 | bytes 6619140 | tf_op jit(solution)/shard_map/dot_general | solution.py:70
  148.4 4.0 %multiply_reduce_fusion.4 = (f32[]{:T(128)}, f32[896,1024]{1,0:T(8,128)}) fusion(bf16[6144,1024]{1,0:T(8,128)(2,1)S(1)} %copy-done.4, bf16[8,768,896]{2,1,0:T(8,128)(2,1)S(1)} %copy-done), kind=kOutput, calls=%fused_computation.6 | convolution fusion | flops 1411121152 | bytes 6619140 | tf_op jit(solution)/shard_map/dot_general | solution.py:70
  152.5 4.1 %multiply_reduce_fusion.5 = (f32[]{:T(128)}, f32[896,1024]{1,0:T(8,128)}) fusion(bf16[6144,1024]{1,0:T(8,128)(2,1)S(1)} %copy-done.4, bf16[8,768,896]{2,1,0:T(8,128)(2,1)S(1)} %copy-done), kind=kOutput, calls=%fused_computation.7 | convolution fusion | flops 1411121152 | bytes 6619140 | tf_op jit(solution)/shard_map/dot_general | solution.py:70
  156.6 4.2 %multiply_reduce_fusion.6 = (f32[]{:T(128)}, f32[896,1024]{1,0:T(8,128)}) fusion(bf16[6144,1024]{1,0:T(8,128)(2,1)S(1)} %copy-done.4, bf16[8,768,896]{2,1,0:T(8,128)(2,1)S(1)} %copy-done), kind=kOutput, calls=%fused_computation.8 | convolution fusion | flops 1411121152 | bytes 6619140 | tf_op jit(solution)/shard_map/dot_general | solution.py:70
  160.7 4.2 %multiply_reduce_fusion.7 = (f32[]{:T(128)}, f32[896,1024]{1,0:T(8,128)}) fusion(bf16[6144,1024]{1,0:T(8,128)(2,1)S(1)} %copy-done.4, bf16[8,768,896]{2,1,0:T(8,128)(2,1)S(1)} %copy-done), kind=kOutput, calls=%fused_computation.9 | convolution fusion | flops 1411121152 | bytes 6619140 | tf_op jit(solution)/shard_map/dot_general | solution.py:70
  164.9 4.4 %multiply_reduce_fusion = (f32[]{:T(128)}, f32[896,1024]{1,0:T(8,128)}) fusion(bf16[6144,1024]{1,0:T(8,128)(2,1)S(1)} %copy-done.4, bf16[8,768,896]{2,1,0:T(8,128)(2,1)S(1)} %copy-done), kind=kOutput, calls=%fused_computation.2 | convolution fusion | flops 1411121152 | bytes 6619140 | tf_op jit(solution)/shard_map/dot_general | solution.py:70
  169.2 5.1 %stack.71 = f32[8]{0:T(128)S(1)} concatenate(f32[1]{0:T(128)} %bitcast.10, f32[1]{0:T(128)} %bitcast.12, f32[1]{0:T(128)} %bitcast.14, f32[1]{0:T(128)} %bitcast.16, f32[1]{0:T(128)} %bitcast.18, f32[1]{0:T(128)} %bitcast.20, f32[1]{0:T(128)} %bitcast.22, f32[1]{0:T(128)} %bitcast.24), dimensions={0} | concatenate | bytes 64 | tf_op jit(solution)/shard_map/stack | solution.py:75
  174.3 0.0 collective-permute-start.7
  174.4 1.1 collective-permute-done.7
  175.5 2.7 %collective-permute-start.10 = (f32[8]{0:T(128)S(1)}, f32[8]{0:T(128)S(1)}, u32[]{:S(2)}, u32[]{:S(2)}) collective-permute-start(f32[8]{0:T(128)S(1)} %add.114), channel_id=1, source_target_pairs={{0,6},{1,7},{2,4},{3,5},{4,2},{5,3},{6,0},{7,1},{8,14},{9,15},{10,... | collective-permute-start | bytes 104 | tf_op jit(solution)/shard_map/ppermute | solution.py:20
  178.2 0.8 collective-permute-start.9
  179.1 0.6 collective-permute-start.8
  179.6 0.7 collective-permute-done.10
  180.3 3.0 %collective-permute-done.9 = f32[8]{0:T(128)S(1)} collective-permute-done((f32[8]{0:T(128)S(1)}, f32[8]{0:T(128)S(1)}, u32[]{:S(2)}, u32[]{:S(2)}) %collective-permute-start.9) | collective-permute-done | bytes 64 | tf_op jit(solution)/shard_map/ppermute | solution.py:20
  183.3 0.0 collective-permute-done.8
  183.3 1.3 collective-permute-start.13
  184.6 2.7 %collective-permute-start.12 = (f32[8]{0:T(128)S(1)}, f32[8]{0:T(128)S(1)}, u32[]{:S(2)}, u32[]{:S(2)}) collective-permute-start(f32[8]{0:T(128)S(1)} %add_add_fusion.2), channel_id=1, source_target_pairs={{0,128},{8,136},{16,144},{24,152},{32,160},{40,168},{48,176},{56,1... | collective-permute-start | bytes 104 | tf_op jit(solution)/shard_map/ppermute | solution.py:20
  187.3 0.2 collective-permute-start.11
  187.5 0.0 collective-permute-done.13
  187.5 2.2 collective-permute-done.12
  189.6 1.2 collective-permute-done.11
  190.8 3.0 %collective-permute-start.16 = (f32[8]{0:T(128)S(1)}, f32[8]{0:T(128)S(1)}, u32[]{:S(2)}, u32[]{:S(2)}) collective-permute-start(f32[8]{0:T(128)S(1)} %add_add_fusion.1), channel_id=1, source_target_pairs={{0,24},{8,16},{16,8},{24,0},{32,56},{40,48},{48,40},{56,32},{64,88... | collective-permute-start | bytes 104 | tf_op jit(solution)/shard_map/ppermute | solution.py:20
  193.8 0.0 collective-permute-start.15
  193.8 1.4 collective-permute-start.14
  195.2 1.0 collective-permute-done.16
  196.2 2.1 collective-permute-done.15
  198.3 0.0 collective-permute-done.14
  198.3 2.0 collective-permute-start.17
  200.3 5.5 %collective-permute-done.17 = f32[8]{0:T(128)S(1)} collective-permute-done((f32[8]{0:T(128)S(1)}, f32[8]{0:T(128)S(1)}, u32[]{:S(2)}, u32[]{:S(2)}) %collective-permute-start.17) | collective-permute-done | bytes 64 | tf_op jit(solution)/shard_map/ppermute | solution.py:20
  205.9 0.5 add_divide_fusion
  206.4 0.7 fusion.21
  207.1 17.5 %multiply_convert_fusion = bf16[896,1024]{1,0:T(8,128)(2,1)} fusion(f32[896,1024]{1,0:T(8,128)} %get-tuple-element.27, f32[896,1024]{1,0:T(8,128)} %get-tuple-element.25, f32[896,1024]{1,0:T(8,128)} %get-tuple-element.23, f32[896,1024]{1,0:T(8,128)} %get-tuple-element.21, f32[896,1024]{1,0:T(8,128)} %get-tuple-element.19, f32[896,1024]{1,0:T(8,128)} %get-tuple-element.17, ...), kind=kLoop, calls=%fused_computation.1 | loop fusion | flops 15597568 | bytes 31195168 | tf_op jit(solution)/shard_map/convert_element_type | solution.py:81
  (16 shorter events, 0.1 us)
Async XLA Ops:
  7.2 123.9 %all-gather.2.cloned.1.call-start = ((), (), s32[]{:S(2)}) async-start(), calls=%async_computation | async-start | bytes 12976128 | tf_op jit(solution)/shard_map/all_gather | solution.py:51
  9.9 19.2 %collective-permute-start = (bf16[768,896]{1,0:T(8,128)(2,1)}, bf16[768,896]{1,0:T(8,128)(2,1)S(1)}, u32[]{:S(2)}, u32[]{:S(2)}) collective-permute-start(bf16[768,896]{1,0:T(8,128)(2,1)} %param.3), channel_id=1, source_target_pairs={{0,1},{1,2},{2,3},{3,4},{4,5},{5,6},{6,7},{7,0},{8,9},{9,10},{10,1... | collective-permute-start | bytes 4128776 | tf_op jit(solution)/shard_map/ppermute | solution.py:58
  29.0 18.9 %collective-permute-start.1 = (bf16[768,896]{1,0:T(8,128)(2,1)S(1)}, bf16[768,896]{1,0:T(8,128)(2,1)S(1)}, u32[]{:S(2)}, u32[]{:S(2)}) collective-permute-start(bf16[768,896]{1,0:T(8,128)(2,1)S(1)} %collective-permute-done), channel_id=1, source_target_pairs={{0,1},{1,2},{2,3},{3,4},{4,5},{5,6},{6,7},{7,0},{8,9},{9,10},{10,1... | collective-permute-start | bytes 4128776 | tf_op jit(solution)/shard_map/ppermute | solution.py:58
  29.0 19.1 %collective-permute-start.4 = (bf16[768,896]{1,0:T(8,128)(2,1)}, bf16[768,896]{1,0:T(8,128)(2,1)S(1)}, u32[]{:S(2)}, u32[]{:S(2)}) collective-permute-start(bf16[768,896]{1,0:T(8,128)(2,1)} %param.3), channel_id=1, source_target_pairs={{1,0},{2,1},{3,2},{4,3},{5,4},{6,5},{7,6},{0,7},{9,8},{10,9},{11,1... | collective-permute-start | bytes 4128776 | tf_op jit(solution)/shard_map/ppermute | solution.py:60
  48.0 1.1 copy-start.2
  48.0 19.1 %collective-permute-start.2 = (bf16[768,896]{1,0:T(8,128)(2,1)S(1)}, bf16[768,896]{1,0:T(8,128)(2,1)}, u32[]{:S(2)}, u32[]{:S(2)}) collective-permute-start(bf16[768,896]{1,0:T(8,128)(2,1)S(1)} %collective-permute-done.1), channel_id=1, source_target_pairs={{0,1},{1,2},{2,3},{3,4},{4,5},{5,6},{6,7},{7,0},{8,9},{9,10},{10,1... | collective-permute-start | bytes 4128776 | tf_op jit(solution)/shard_map/ppermute | solution.py:58
  49.1 18.1 %collective-permute-start.5 = (bf16[768,896]{1,0:T(8,128)(2,1)S(1)}, bf16[768,896]{1,0:T(8,128)(2,1)}, u32[]{:S(2)}, u32[]{:S(2)}) collective-permute-start(bf16[768,896]{1,0:T(8,128)(2,1)S(1)} %collective-permute-done.4), channel_id=1, source_target_pairs={{1,0},{2,1},{3,2},{4,3},{5,4},{6,5},{7,6},{0,7},{9,8},{10,9},{11,1... | collective-permute-start | bytes 4128776 | tf_op jit(solution)/shard_map/ppermute | solution.py:60
  67.0 19.3 %collective-permute-start.3 = (bf16[768,896]{1,0:T(8,128)(2,1)}, bf16[768,896]{1,0:T(8,128)(2,1)}, u32[]{:S(2)}, u32[]{:S(2)}) collective-permute-start(bf16[768,896]{1,0:T(8,128)(2,1)} %collective-permute-done.2), channel_id=1, source_target_pairs={{0,1},{1,2},{2,3},{3,4},{4,5},{5,6},{6,7},{7,0},{8,9},{9,10},{10,1... | collective-permute-start | bytes 4128776 | tf_op jit(solution)/shard_map/ppermute | solution.py:58
  67.0 24.5 %copy-start.3 = (bf16[768,896]{1,0:T(8,128)(2,1)S(1)}, bf16[768,896]{1,0:T(8,128)(2,1)}, u32[]{:S(2)}) copy-start(bf16[768,896]{1,0:T(8,128)(2,1)} %copy-done.2) | copy-start | bytes 4128772
  67.2 31.7 %collective-permute-start.6 = (bf16[768,896]{1,0:T(8,128)(2,1)}, bf16[768,896]{1,0:T(8,128)(2,1)S(1)}, u32[]{:S(2)}, u32[]{:S(2)}) collective-permute-start(bf16[768,896]{1,0:T(8,128)(2,1)} %collective-permute-done.5), channel_id=1, source_target_pairs={{1,0},{2,1},{3,2},{4,3},{5,4},{6,5},{7,6},{0,7},{9,8},{10,9},{11,1... | collective-permute-start | bytes 4128776 | tf_op jit(solution)/shard_map/ppermute | solution.py:60
  88.9 5.1 %copy-start.1 = (bf16[768,896]{1,0:T(8,128)(2,1)S(1)}, bf16[768,896]{1,0:T(8,128)(2,1)}, u32[]{:S(2)}) copy-start(bf16[768,896]{1,0:T(8,128)(2,1)} %param.3) | copy-start | bytes 4128772
  131.1 6.0 %copy-start = (bf16[8,768,896]{2,1,0:T(8,128)(2,1)S(1)}, bf16[8,768,896]{2,1,0:T(8,128)(2,1)}, u32[]{:S(2)}) copy-start(bf16[8,768,896]{2,1,0:T(8,128)(2,1)} %gather_fusion) | copy-start | bytes 33030148
  137.1 11.3 %copy-start.4 = (bf16[6144,1024]{1,0:T(8,128)(2,1)S(1)}, bf16[6144,1024]{1,0:T(8,128)(2,1)}, u32[]{:S(2)}) copy-start(bf16[6144,1024]{1,0:T(8,128)(2,1)} %all-gather.2.cloned.1.call-done) | copy-start | bytes 37748740
  174.3 1.2 collective-permute-start.7
  175.5 4.8 %collective-permute-start.10 = (f32[8]{0:T(128)S(1)}, f32[8]{0:T(128)S(1)}, u32[]{:S(2)}, u32[]{:S(2)}) collective-permute-start(f32[8]{0:T(128)S(1)} %add.114), channel_id=1, source_target_pairs={{0,6},{1,7},{2,4},{3,5},{4,2},{5,3},{6,0},{7,1},{8,14},{9,15},{10,... | collective-permute-start | bytes 104 | tf_op jit(solution)/shard_map/ppermute | solution.py:20
  178.2 5.1 %collective-permute-start.9 = (f32[8]{0:T(128)S(1)}, f32[8]{0:T(128)S(1)}, u32[]{:S(2)}, u32[]{:S(2)}) collective-permute-start(f32[8]{0:T(128)S(1)} %add.114), channel_id=1, source_target_pairs={{0,4},{1,5},{2,6},{3,7},{4,0},{5,1},{6,2},{7,3},{8,12},{9,13},{10,... | collective-permute-start | bytes 104 | tf_op jit(solution)/shard_map/ppermute | solution.py:20
  179.1 4.2 %collective-permute-start.8 = (f32[8]{0:T(128)S(1)}, f32[8]{0:T(128)S(1)}, u32[]{:S(2)}, u32[]{:S(2)}) collective-permute-start(f32[8]{0:T(128)S(1)} %add.114), channel_id=1, source_target_pairs={{0,2},{1,3},{2,0},{3,1},{4,6},{5,7},{6,4},{7,5},{8,10},{9,11},{10,... | collective-permute-start | bytes 104 | tf_op jit(solution)/shard_map/ppermute | solution.py:20
  183.3 4.2 %collective-permute-start.13 = (f32[8]{0:T(128)S(1)}, f32[8]{0:T(128)S(1)}, u32[]{:S(2)}, u32[]{:S(2)}) collective-permute-start(f32[8]{0:T(128)S(1)} %add_add_fusion.2), channel_id=1, source_target_pairs={{0,192},{8,200},{16,208},{24,216},{32,224},{40,232},{48,240},{56,2... | collective-permute-start | bytes 104 | tf_op jit(solution)/shard_map/ppermute | solution.py:20
  184.6 5.1 %collective-permute-start.12 = (f32[8]{0:T(128)S(1)}, f32[8]{0:T(128)S(1)}, u32[]{:S(2)}, u32[]{:S(2)}) collective-permute-start(f32[8]{0:T(128)S(1)} %add_add_fusion.2), channel_id=1, source_target_pairs={{0,128},{8,136},{16,144},{24,152},{32,160},{40,168},{48,176},{56,1... | collective-permute-start | bytes 104 | tf_op jit(solution)/shard_map/ppermute | solution.py:20
  187.3 3.6 %collective-permute-start.11 = (f32[8]{0:T(128)S(1)}, f32[8]{0:T(128)S(1)}, u32[]{:S(2)}, u32[]{:S(2)}) collective-permute-start(f32[8]{0:T(128)S(1)} %add_add_fusion.2), channel_id=1, source_target_pairs={{0,64},{8,72},{16,80},{24,88},{32,96},{40,104},{48,112},{56,120},{... | collective-permute-start | bytes 104 | tf_op jit(solution)/shard_map/ppermute | solution.py:20
  190.8 5.4 %collective-permute-start.16 = (f32[8]{0:T(128)S(1)}, f32[8]{0:T(128)S(1)}, u32[]{:S(2)}, u32[]{:S(2)}) collective-permute-start(f32[8]{0:T(128)S(1)} %add_add_fusion.1), channel_id=1, source_target_pairs={{0,24},{8,16},{16,8},{24,0},{32,56},{40,48},{48,40},{56,32},{64,88... | collective-permute-start | bytes 104 | tf_op jit(solution)/shard_map/ppermute | solution.py:20
  193.8 4.5 %collective-permute-start.15 = (f32[8]{0:T(128)S(1)}, f32[8]{0:T(128)S(1)}, u32[]{:S(2)}, u32[]{:S(2)}) collective-permute-start(f32[8]{0:T(128)S(1)} %add_add_fusion.1), channel_id=1, source_target_pairs={{0,16},{8,24},{16,0},{24,8},{32,48},{40,56},{48,32},{56,40},{64,80... | collective-permute-start | bytes 104 | tf_op jit(solution)/shard_map/ppermute | solution.py:20
  193.8 4.5 %collective-permute-start.14 = (f32[8]{0:T(128)S(1)}, f32[8]{0:T(128)S(1)}, u32[]{:S(2)}, u32[]{:S(2)}) collective-permute-start(f32[8]{0:T(128)S(1)} %add_add_fusion.1), channel_id=1, source_target_pairs={{0,8},{8,0},{16,24},{24,16},{32,40},{40,32},{48,56},{56,48},{64,72... | collective-permute-start | bytes 104 | tf_op jit(solution)/shard_map/ppermute | solution.py:20
  198.3 7.6 %collective-permute-start.17 = (f32[8]{0:T(128)S(1)}, f32[8]{0:T(128)S(1)}, u32[]{:S(2)}, u32[]{:S(2)}) collective-permute-start(f32[8]{0:T(128)S(1)} %add_add_fusion), channel_id=1, source_target_pairs={{0,32},{8,40},{16,48},{24,56},{32,0},{40,8},{48,16},{56,24},{64,96... | collective-permute-start | bytes 104 | tf_op jit(solution)/shard_map/ppermute | solution.py:20
Sparse Core Ops, SparseCore 0:
  10.5 120.4 all-gather.1
